TPU v7x, 32 devices: a whole 2x2x4 slice. The times are simulated.
32 devices in a mesh: ex: 8 (over y, x, core), feat: 4 (over z).
Axes of the slice: x: 2, y: 2, z: 4, core: 2. Of those that a mesh axis runs over, the one named last changes fastest.
Arguments:
- activations: bfloat16 [512, 64, 4096], P('ex', None, 'feat'), may hold values from -6 to 6
- output_gradient_rows: bfloat16 [512, 64, 4096], P('ex', None, 'feat'), may hold values from -6 to 6
- adapter_down_matrix: bfloat16 [4096, 128], P('feat'), may hold values from -0.09375 to 0.09375
- rank_side_sketch: bfloat16 [128, 64], replicated, may hold values from -0.5 to 0.5
- output_side_sketch: bfloat16 [4096, 128], P('feat'), may hold values from -0.09375 to 0.09375
- heldout_gradient_features: float32 [256, 8192], P('ex', 'feat'), may hold values from -6 to 6
- heldout_language_permutation: int32 [256], P('ex'), may hold values from 0 to 255, each once
Outputs:
- scores: float32 [512, 64], P('ex')
Inputs may be any that keep to these rules, and one draw needn't show every extreme that they name: `heldout_language_permutation`: every value of 0 to 255 appears once, so every language has 4 validation examples.
All inputs are finite; a program needn't handle non-finite values.
Results may differ from a plain program's by a relative error of at most 0.0029.
Values sent between devices are 32-bit elements; how exact they have to be, the bound alone decides.
No kernel may reach another device: no remote copies, remote signals or barrier semaphores. Data moves between devices by JAX's collectives and lax.ppermute only.
A program may use at most 64 MiB of HBM per device.

v0:
```python
import jax
import jax.numpy as jnp
from jax import lax
from jax.sharding import PartitionSpec as P

KF = 8192
LANGS = 64


def shards(
    activations,
    output_gradient_rows,
    adapter_down_matrix,
    rank_side_sketch,
    output_side_sketch,
    heldout_gradient_features,
    heldout_language_permutation,
):
    highest = lax.Precision.HIGHEST
    ex_dev = activations.shape[0]
    down_projection_name = jnp.dot(
        adapter_down_matrix, rank_side_sketch, preferred_element_type=jnp.float32
    ).astype(jnp.bfloat16)
    rank_part = jnp.einsum(
        "esd,dr->esr", activations, down_projection_name, preferred_element_type=jnp.float32
    )
    rank_side = lax.psum(rank_part, "feat")
    out_part = jnp.einsum(
        "esd,dk->esk", output_gradient_rows, output_side_sketch, preferred_element_type=jnp.float32
    )
    out_side = lax.psum_scatter(out_part, "feat", scatter_dimension=2, tiled=True)
    grad_feat = jnp.einsum("esk,esr->ekr", out_side, rank_side, precision=highest).reshape(
        ex_dev, -1
    )
    val_square = lax.psum(
        jnp.sum(heldout_gradient_features * heldout_gradient_features, axis=1), "feat"
    )
    val_unit = heldout_gradient_features * lax.rsqrt(val_square + 1e-06)[:, None]
    lang = heldout_language_permutation % LANGS
    onehot = (lang[:, None] == jnp.arange(LANGS, dtype=jnp.int32)[None, :]).astype(jnp.float32)
    lang_part = jnp.dot(onehot.T, val_unit, precision=highest)
    lang_mean = lax.psum(lang_part, "ex") / (
        heldout_language_permutation.shape[0] * lax.axis_size("ex") // LANGS
    )
    inner_part = jnp.dot(grad_feat, lang_mean.T, precision=highest)
    square_part = jnp.sum(grad_feat * grad_feat, axis=1)
    inner, squares = lax.psum((inner_part, square_part), "feat")
    per_lang = heldout_language_permutation.shape[0] * lax.axis_size("ex") // LANGS
    scale = jnp.sqrt(jnp.float32(KF * per_lang))
    return scale * inner * lax.rsqrt(squares + 1e-06)[:, None]


def solution(mesh):
    placed = (
        P("ex", None, "feat"),
        P("ex", None, "feat"),
        P("feat", None),
        P(),
        P("feat", None),
        P("ex", "feat"),
        P("ex"),
    )
    return jax.shard_map(
        shards, mesh=mesh, in_specs=placed, out_specs=P("ex", None), check_vma=False
    )
```

profile of v0, /device:TPU:0, one launch (start us, length us, event | category | flops | bytes accessed | tf_op | source)
XLA Modules:
  0.0 268.0 jit_solution(1419638174889042181)
XLA Ops:
  6.5 0.0 copy-start
  6.5 0.0 all-reduce.4.cloned.1.call-start
  6.5 7.4 %convolution_bitcast_fusion = f32[64,64,64]{2,1,0:T(8,128)} fusion(bf16[64,64,1024]{2,1,0:T(8,128)(2,1)} %param.7, bf16[1024,128]{1,0:T(8,128)(2,1)} %param.9, bf16[128,64]{0,1:T(8,128)(2,1)} %param.10), kind=kOutput, calls=%fused_computation | convolution fusion | flops 553713664 | bytes 9715712 | tf_op jit(solution)/shard_map/esd,dr->esr/dot_general | solution.py:24
  14.0 0.0 all-reduce.4.cloned.1.call-update
  14.0 0.0 copy-start.1
  14.0 0.0 copy-start.2
  14.0 0.0 reduce-scatter.2.cloned.1.call-start
  14.1 0.0 copy-done
  14.1 9.5 %fusion.3 = f32[64,64,128]{1,2,0:T(8,128)} fusion(bf16[64,64,1024]{2,1,0:T(8,128)(2,1)} %param.8, bf16[1024,128]{1,0:T(8,128)(2,1)S(1)} %copy-done), kind=kOutput, calls=%fused_computation.6 | convolution fusion | flops 1073741824 | bytes 10747904 | tf_op jit(solution)/shard_map/esd,dk->esk/dot_general | solution.py:28
  23.5 0.0 reduce-scatter.2.cloned.1.call-update
  23.6 0.0 all-reduce.6.cloned.1.call-start
  23.6 0.0 copy-done.1
  23.6 0.1 multiply_reduce_fusion.1
  23.7 14.1 %psum.36 = f32[32]{0:T(128)S(1)} all-reduce(f32[32]{0:T(128)S(1)} %multiply_reduce_fusion.1), channel_id=1, replica_groups=mesh['ex'=8,'feat'=4] {'feat'}, use_global_device_ids=true, to_apply=%region_3.0 | all-reduce | flops 32 | bytes 256 | tf_op jit(solution)/shard_map/psum | solution.py:35
  37.8 0.0 copy-done.2
  37.8 1.3 fusion.6
  39.1 0.0 all-reduce.6.cloned.1.call-update
  39.1 64.1 %all-reduce.4.cloned.1.call-done = f32[64,64,64]{2,1,0:T(8,128)} async-done(((f32[64,64,64]{2,1,0:T(8,128)}), f32[64,64,64]{2,1,0:T(8,128)}) %all-reduce.4.cloned.1.call-update) | async-done | bytes 1048592 | tf_op jit(solution)/shard_map/psum | solution.py:27
  103.3 78.1 %reduce-scatter.2.cloned.1.call-done = f32[64,64,32]{1,2,0:T(8,128)} async-done(((f32[64,64,128]{1,2,0:T(8,128)}), f32[64,64,32]{1,2,0:T(8,128)}) %reduce-scatter.2.cloned.1.call-update) | async-done | bytes 524304 | tf_op jit(solution)/shard_map/reduce_scatter | solution.py:31
  181.4 4.2 %multiply_reduce_fusion = (f32[64]{0:T(128)S(1)}, f32[64,32,64]{2,1,0:T(8,128)S(1)}) fusion(f32[64,64,32]{1,2,0:T(8,128)} %reduce-scatter.2.cloned.1.call-done, f32[64,64,64]{2,1,0:T(8,128)} %all-reduce.4.cloned.1.call-done), kind=kOutput, calls=%fused_computation.3 | convolution fusion | flops 100925376 | bytes 2097408 | tf_op jit(solution)/shard_map/esk,esr->ekr/dot_general | solution.py:32
  185.6 0.4 reshape.6
  186.0 53.9 %all-reduce.6.cloned.1.call-done = f32[64,2048]{1,0:T(8,128)} async-done(((f32[64,2048]{1,0:T(8,128)}), f32[64,2048]{1,0:T(8,128)}) %all-reduce.6.cloned.1.call-update) | async-done | bytes 524304 | tf_op jit(solution)/shard_map/psum | solution.py:42
  239.9 1.6 fusion.1
  241.5 19.3 %all-reduce = (f32[64,64]{1,0:T(8,128)S(1)}, f32[64]{0:T(128)S(1)}) all-reduce(f32[64,64]{1,0:T(8,128)S(1)} %fusion.1, f32[64]{0:T(128)S(1)} %get-tuple-element.7), channel_id=1, replica_groups=mesh['ex'=8,'feat'=4] {'feat'}, use_global_device_ids=true, to_apply=%region_5.6 | all-reduce | flops 4160 | bytes 33280 | tf_op jit(solution)/shard_map/psum | solution.py:47
  260.8 0.7 broadcast_multiply_fusion
  (3 shorter events, 0.0 us)
Async XLA Ops:
  6.5 7.5 %copy-start = (bf16[1024,128]{1,0:T(8,128)(2,1)S(1)}, bf16[1024,128]{1,0:T(8,128)(2,1)}, u32[]{:S(2)}) copy-start(bf16[1024,128]{1,0:T(8,128)(2,1)} %param.11) | copy-start | bytes 786436
  6.5 96.7 %all-reduce.4.cloned.1.call-start = ((), (), s32[]{:S(2)}) async-start(), calls=%async_computation.2 | async-start | bytes 4194304 | tf_op jit(solution)/shard_map/psum | solution.py:27
  14.0 9.6 %copy-start.1 = (f32[32,2048]{1,0:T(8,128)S(1)}, f32[32,2048]{1,0:T(8,128)}, u32[]{:S(2)}) copy-start(f32[32,2048]{1,0:T(8,128)} %param.12) | copy-start | bytes 786436
  14.0 23.8 %copy-start.2 = (s32[32]{0:T(128)S(1)}, s32[32]{0:T(128)}, u32[]{:S(2)}) copy-start(s32[32]{0:T(128)} %param.13) | copy-start | bytes 388
  14.0 167.4 %reduce-scatter.2.cloned.1.call-start = ((), (), s32[]{:S(2)}) async-start(), calls=%async_computation.1 | async-start | bytes 5242880 | tf_op jit(solution)/shard_map/reduce_scatter | solution.py:31
  23.6 216.3 %all-reduce.6.cloned.1.call-start = ((), (), s32[]{:S(2)}) async-start(), calls=%async_computation.3 | async-start | bytes 1048576 | tf_op jit(solution)/shard_map/psum | solution.py:42
Sparse Core Ops, SparseCore 0:
  14.1 89.1 all-reduce.3
  105.6 75.8 reduce-scatter.1
  184.5 55.3 all-reduce.5
where the time goes:
time: 268 us
  waiting for transfers between devices  196 us (73%)
  blocking collectives  33.3 us (12%)
  matrix products  23.9 us (9%)
  between operations  13.2 us (5%)
    reduce_scatter x1, waiting for transfers between devices, shards(): lax.psum_scatter(out_part, 'feat', scatter_dimension=2, tiled=True)  78.1 us
    psum x1, waiting for transfers between devices, shards(): rank_side = lax.psum(rank_part, 'feat')  64.1 us
    psum x1, waiting for transfers between devices, shards(): lax.psum(lang_part, 'ex')  53.9 us
    psum x1, blocking collectives, shards(): inner, squares = lax.psum((inner_part, square_part), 'feat')  19.3 us
    psum x1, blocking collectives, shards(): lax.psum(jnp.sum(heldout_gradient_features * heldout_gradient_features, a...  14.1 us
    dot_general x1, matrix products, shards(): jnp.einsum('esd,dk->esk', output_gradient_rows, output_side_sketch, prefe...  9.45 us
    dot_general x1, matrix products, shards(): jnp.einsum('esd,dr->esr', activations, down_projection_name, preferred_el...  7.42 us
  transfers between devices with their start and end apart: 3, of which 3 were waited for; matrix products, arithmetic and copies ran while one was open for 6% of the time, Pallas kernels for 0%

commit v1 on v0

--- a/solution.py
+++ b/solution.py
@@ -1,3 +1,4 @@
+import functools
 import jax
 import jax.numpy as jnp
 from jax import lax
@@ -5,6 +6,14 @@
 
 KF = 8192
 LANGS = 64
+
+
+def loops_begin(raw, a_name):
+    f_next = lax.all_gather(raw, axis_name=a_name).sum(axis=0)
+    return f_next
+
+
+field_pack = functools.partial(loops_begin, a_name="ex")
 
 
 def shards(
@@ -39,7 +48,7 @@
     lang = heldout_language_permutation % LANGS
     onehot = (lang[:, None] == jnp.arange(LANGS, dtype=jnp.int32)[None, :]).astype(jnp.float32)
     lang_part = jnp.dot(onehot.T, val_unit, precision=highest)
-    lang_mean = lax.psum(lang_part, "ex") / (
+    lang_mean = field_pack(lang_part) / (
         heldout_language_permutation.shape[0] * lax.axis_size("ex") // LANGS
     )
     inner_part = jnp.dot(grad_feat, lang_mean.T, precision=highest)

time: 268 us -> 217 us (0.81)
  waiting for transfers between devices: 196 us -> 141 us
    psum x1 -> x0, waiting for transfers between devices: 53.9 us -> none  [shards(): lax.psum(lang_part, 'ex')]
  transfers between devices with their start and end apart: 3 -> 3, of which waited for: 3 -> 2; matrix products, arithmetic and copies ran while one was open for 6% -> 7% of each run, Pallas kernels for 0% -> 0%
where the time goes in v1:
time: 217 us
  waiting for transfers between devices  141 us (65%)
  blocking collectives  32.8 us (15%)
  matrix products  22.9 us (11%)
  between operations  14.9 us (7%)
  other arithmetic  3.34 us (2%)
    reduce_scatter x1, waiting for transfers between devices, shards(): lax.psum_scatter(out_part, 'feat', scatter_dimension=2, tiled=True)  78.1 us
    psum x1, waiting for transfers between devices, shards(): rank_side = lax.psum(rank_part, 'feat')  63.2 us
    psum x1, blocking collectives, shards(): inner, squares = lax.psum((inner_part, square_part), 'feat')  18.6 us
    psum x1, blocking collectives, shards(): lax.psum(jnp.sum(heldout_gradient_features * heldout_gradient_features, a...  14.1 us
    dot_general x1, matrix products, shards(): jnp.einsum('esd,dk->esk', output_gradient_rows, output_side_sketch, prefe...  9.49 us
    dot_general x1, matrix products, shards(): jnp.einsum('esd,dr->esr', activations, down_projection_name, preferred_el...  7.37 us
  transfers between devices with their start and end apart: 3, of which 2 were waited for; matrix products, arithmetic and copies ran while one was open for 7% of the time, Pallas kernels for 0%

profile of v1, /device:TPU:0, one launch (start us, length us, event | category | flops | bytes accessed | tf_op | source)
XLA Modules:
  0.0 216.6 jit_solution(14766126792508833668)
XLA Ops:
  7.4 0.0 copy-start
  7.4 0.0 all-reduce.3.cloned.1.call-start
  7.4 7.4 %convolution_bitcast_fusion = f32[64,64,64]{2,1,0:T(8,128)} fusion(bf16[64,64,1024]{2,1,0:T(8,128)(2,1)} %param.7, bf16[1024,128]{1,0:T(8,128)(2,1)} %param.9, bf16[128,64]{0,1:T(8,128)(2,1)} %param.10), kind=kOutput, calls=%fused_computation | convolution fusion | flops 553713664 | bytes 9715712 | tf_op jit(solution)/shard_map/esd,dr->esr/dot_general | solution.py:33
  14.7 0.0 all-reduce.3.cloned.1.call-update
  14.8 0.0 reduce-scatter.2.cloned.1.call-start
  14.8 0.0 copy-done
  14.8 9.5 %fusion.3 = f32[64,64,128]{1,2,0:T(8,128)} fusion(bf16[64,64,1024]{2,1,0:T(8,128)(2,1)} %param.8, bf16[1024,128]{1,0:T(8,128)(2,1)S(1)} %copy-done), kind=kOutput, calls=%fused_computation.6 | convolution fusion | flops 1073741824 | bytes 10747904 | tf_op jit(solution)/shard_map/esd,dk->esk/dot_general | solution.py:37
  24.3 0.0 copy-start.1
  24.3 0.0 copy-start.2
  24.3 0.0 reduce-scatter.2.cloned.1.call-update
  24.3 0.0 all-gather.3.cloned.1.call-start
  24.4 0.9 copy-done.1
  25.3 0.1 multiply_reduce_fusion.1
  25.4 14.1 %psum.29 = f32[32]{0:T(128)S(1)} all-reduce(f32[32]{0:T(128)S(1)} %multiply_reduce_fusion.1), channel_id=1, replica_groups=mesh['ex'=8,'feat'=4] {'feat'}, use_global_device_ids=true, to_apply=%region_3.0 | all-reduce | flops 32 | bytes 256 | tf_op jit(solution)/shard_map/psum | solution.py:44
  39.5 0.0 copy-done.2
  39.6 1.3 fusion.6
  40.8 0.0 all-gather.3.cloned.1.call-update
  40.9 63.2 %all-reduce.3.cloned.1.call-done = f32[64,64,64]{2,1,0:T(8,128)} async-done(((f32[64,64,64]{2,1,0:T(8,128)}), f32[64,64,64]{2,1,0:T(8,128)}) %all-reduce.3.cloned.1.call-update) | async-done | bytes 1048592 | tf_op jit(solution)/shard_map/psum | solution.py:36
  104.1 78.1 %reduce-scatter.2.cloned.1.call-done = f32[64,64,32]{1,2,0:T(8,128)} async-done(((f32[64,64,128]{1,2,0:T(8,128)}), f32[64,64,32]{1,2,0:T(8,128)}) %reduce-scatter.2.cloned.1.call-update) | async-done | bytes 524304 | tf_op jit(solution)/shard_map/reduce_scatter | solution.py:40
  182.2 4.2 %multiply_reduce_fusion = (f32[64]{0:T(128)S(1)}, f32[64,32,64]{2,1,0:T(8,128)S(1)}) fusion(f32[64,64,32]{1,2,0:T(8,128)} %reduce-scatter.2.cloned.1.call-done, f32[64,64,64]{2,1,0:T(8,128)} %all-reduce.3.cloned.1.call-done), kind=kOutput, calls=%fused_computation.3 | convolution fusion | flops 100925376 | bytes 2097408 | tf_op jit(solution)/shard_map/esk,esr->ekr/dot_general | solution.py:41
  186.4 0.4 reshape.6
  186.7 0.0 all-gather.3.cloned.1.call-done
  186.8 2.5 %reduce_sum.28 = f32[64,2048]{1,0:T(8,128)S(1)} reduce(f32[8,64,2048]{2,1,0:T(8,128)} %bitcast.17, f32[]{:T(128)} %constant.21.clone.1), dimensions={0}, to_apply=%region_4.5 | reduce | flops 917504 | bytes 4718596 | tf_op jit(solution)/shard_map/reduce_sum | solution.py:12
  189.3 0.6 fusion.1
  189.9 18.6 %all-reduce = (f32[64,64]{1,0:T(8,128)S(1)}, f32[64]{0:T(128)S(1)}) all-reduce(f32[64,64]{1,0:T(8,128)S(1)} %fusion.1, f32[64]{0:T(128)S(1)} %get-tuple-element.7), channel_id=1, replica_groups=mesh['ex'=8,'feat'=4] {'feat'}, use_global_device_ids=true, to_apply=%region_5.6 | all-reduce | flops 4160 | bytes 33280 | tf_op jit(solution)/shard_map/psum | solution.py:56
  208.5 0.7 broadcast_multiply_fusion
  (3 shorter events, 0.0 us)
Async XLA Ops:
  7.4 7.5 %copy-start = (bf16[1024,128]{1,0:T(8,128)(2,1)S(1)}, bf16[1024,128]{1,0:T(8,128)(2,1)}, u32[]{:S(2)}) copy-start(bf16[1024,128]{1,0:T(8,128)(2,1)} %param.11) | copy-start | bytes 786436
  7.4 96.7 %all-reduce.3.cloned.1.call-start = ((), (), s32[]{:S(2)}) async-start(), calls=%async_computation.2 | async-start | bytes 4194304 | tf_op jit(solution)/shard_map/psum | solution.py:36
  14.8 167.4 %reduce-scatter.2.cloned.1.call-start = ((), (), s32[]{:S(2)}) async-start(), calls=%async_computation.1 | async-start | bytes 5242880 | tf_op jit(solution)/shard_map/reduce_scatter | solution.py:40
  24.3 0.9 copy-start.1
  24.3 15.2 %copy-start.2 = (s32[32]{0:T(128)S(1)}, s32[32]{0:T(128)}, u32[]{:S(2)}) copy-start(s32[32]{0:T(128)} %param.13) | copy-start | bytes 388
  24.3 162.4 %all-gather.3.cloned.1.call-start = ((), (), s32[]{:S(2)}) async-start(), calls=%async_computation.3 | async-start | bytes 4718592 | tf_op jit(solution)/shard_map/all_gather | solution.py:12
Sparse Core Ops, SparseCore 0:
  14.9 89.1 all-reduce.2
  106.3 75.8 reduce-scatter.1
Sparse Core Ops, SparseCore 1:
  40.9 34.6 all-gather.2
